TPU v7x, 32 devices: a whole 2x2x4 slice. The times are simulated.
32 devices in a mesh: band: 2 (over x), row: 16 (over z, y, core).
Axes of the slice: x: 2, y: 2, z: 4, core: 2. Of those that a mesh axis runs over, the one named last changes fastest.
Arguments:
- spectra: float32 [2, 16, 4096, 256], P(None, None, 'row', 'band'), parts along dimension 3, may hold values from -6 to 6
- coda_bins: int32 [8], P('band'), parts along dimension 0, may hold values from 0 to 15
- source_mask: int32 [128, 64], P('band'), parts along dimension 0, may hold values 0 or 1
Outputs:
- third_order: float32 [8192, 2, 4, 128], P(('band', 'row')), parts along dimension 0
There are 2 independent parts, one for each index of `band`. A program takes and returns all parts, laid end to end along the dimension named above; each array names one. Nothing has to cross between parts.
Inputs may be any that keep to these rules, and one draw needn't show every extreme that they name: `coda_bins`: each entry is a bin of the band's spectrum; entries may repeat.
All inputs are finite; a program needn't handle non-finite values.
Results may differ from a plain program's by a relative error of at most 0.004.
Values may be sent and summed in bfloat16 or wider, within the bound.
No kernel may reach another device: no remote copies, remote signals or barrier semaphores. Data moves between devices by JAX's collectives and lax.ppermute only.
A program may use at most 128 MiB of HBM per device.

v0:
```python
import functools

import jax
import jax.numpy as jnp
from jax import lax
from jax.experimental import pallas as pl
from jax.experimental.pallas import tpu as pltpu
from jax.sharding import PartitionSpec as P


NTGT = 128
NT_DIMS = (((1,), (1,)), ((), ()))
F32, BF16 = jnp.float32, jnp.bfloat16
VMEM = pl.BlockSpec(memory_space=pltpu.VMEM)
SMEM = pl.BlockSpec(memory_space=pltpu.SMEM)
ANY = pl.BlockSpec(memory_space=pl.ANY)


def ready(layout, mask, packed, wanted):
    _, _, own, spacing, grp = layout
    per, groups = own // grp, mask.shape[0]
    values = mask[...].astype(F32).astype(BF16)
    group = lax.broadcasted_iota(jnp.int32, (groups, 128), 0)
    column = lax.broadcasted_iota(jnp.int32, (groups, 128), 1)
    bit = lax.shift_left(jnp.int32(1), group & (per - 1))
    here = lax.shift_right_logical(group, per.bit_length() - 1) == column
    weight = jnp.where(here, bit, 0).astype(F32).astype(BF16)
    packed[...] = jnp.dot(values, weight, preferred_element_type=F32).astype(jnp.int32)
    rows_of = lax.broadcasted_iota(jnp.int32, (NTGT, groups), 0)
    rowg = lax.shift_right_logical(rows_of, (grp // spacing).bit_length() - 1)
    rowpick = (rowg == lax.broadcasted_iota(jnp.int32, rowg.shape, 1)).astype(F32).astype(BF16)
    values = jnp.concatenate([values, jnp.zeros((groups, 128), BF16)], axis=1)[:, :128]
    wanted[...] = jnp.dot(rowpick, values, preferred_element_type=F32)


def whiten_kernel(layout, bins, spectra, mask, *refs):
    count, spread = layout[:2]
    outs, (packed, wanted, held, sems, near_mask, mask_sem) = refs[:count], refs[count:]
    mine = lax.axis_index("row") // spread
    fetch = pltpu.make_async_copy(mask, near_mask, mask_sem)
    copies = [
        pltpu.make_async_copy(spectra.at[:, bins[mine ^ slot]], held.at[slot], sems.at[slot])
        for slot in range(count)
    ]
    for copy in (*copies, fetch):
        copy.start()
    for slot in range(count):
        copies[slot].wait()
        real, imag = held[slot, 0], held[slot, 1]
        power = jnp.mean(real * real + imag * imag, axis=1, keepdims=True)
        scale = 1.0 / jnp.sqrt(power + 1e-06)
        outs[slot][...] = jnp.concatenate([real * scale, imag * scale], axis=1).astype(BF16)
    fetch.wait()
    ready(layout, near_mask, packed, wanted)


def whiten(spectra, bins, mask, layout):
    _, _, own, windows = spectra.shape
    count = bins.shape[0]
    return pl.pallas_call(
        functools.partial(whiten_kernel, layout),
        in_specs=[SMEM, ANY, ANY],
        out_specs=[VMEM] * (count + 2),
        out_shape=[pltpu.VMEM((own, 2 * windows), BF16)] * count
        + [pltpu.VMEM((mask.shape[0], 128), jnp.int32), pltpu.VMEM((NTGT, 128), F32)],
        scratch_shapes=[
            pltpu.VMEM((count, 2, own, windows), F32),
            pltpu.SemaphoreType.DMA((count,)),
            pltpu.VMEM(mask.shape, jnp.int32),
            pltpu.SemaphoreType.DMA,
        ],
        name="whiten",
    )(bins, spectra, mask)


def quarter_turn(rows):
    half = rows.shape[1] // 2
    return jnp.concatenate([-rows[:, half:], rows[:, :half]], axis=1)


def source_row(spread, slot, held):
    me = lax.axis_index("row")
    return ((me // spread) ^ slot) * spread + ((me % spread) ^ held)


def table_place(layout, slot, held):
    count, _, own, _, grp = layout
    part = count // 2
    return slot // part, (held * part + slot % part) * (1 << (own // grp))


def receive(layout, slots, tables, table, right, lefts, outs):
    count, spread, own, _, grp = layout
    per, width = own // grp, right.shape[-1]
    half = width // 2

    def receiver_body(at, carry):
        slot = slots[0] + lax.shift_right_logical(at, per.bit_length() - 1)
        receiver = source_row(spread, slot, 0) * per + (at & (per - 1))
        total = None
        for held in range(spread):
            for piece in range(count):
                bits = table[receiver, source_row(spread, piece, held)]
                which, base = table_place(layout, piece, held)
                term = tables[which][jnp.where(bits == 0, 0, bits + base)]
                total = term if total is None else total + term
        right[at, 0:NTGT] = total.astype(BF16)
        right[at, NTGT:] = quarter_turn(total).astype(BF16)
        return carry

    lax.fori_loop(0, len(slots) * per, receiver_body, 0)
    for at in range(len(slots)):
        for part in range(per):
            rows = pl.ds(part * grp, grp)
            result = lax.dot_general(
                lefts[at][rows, :], right[at * per + part], NT_DIMS, preferred_element_type=F32
            )
            outs[at][rows, :] = (result * (1.0 / (half * half))).astype(BF16)


def third_kernel(layout, slots, packed, wanted, *refs):
    count, spread, own, spacing, grp = layout
    blocks, refs = refs[: count * spread], refs[count * spread :]
    tables, refs = refs[:2], refs[2:]
    outs, refs = refs[: len(slots)], refs[len(slots) :]
    everyone, trows, targets, right, table, sem = refs
    copy = pltpu.make_async_copy(packed, table, sem)
    copy.start()
    per, tper = own // grp, own // spacing
    tile, duo = 16, min(2, own // grp)
    span = duo * grp
    for held in range(spread):
        for slot in range(count):
            block = blocks[slot * spread + held]
            everyone[held * count + slot] = block[...]
            row = source_row(spread, slot, held)
            for j in range(tper):
                trows[pl.ds(row * tper + j, 1), :] = block[pl.ds(j * spacing, 1), :].astype(F32)
    value = trows[...].astype(BF16)
    targets[0:NTGT] = value
    targets[NTGT:] = -quarter_turn(value)
    for one in tables:
        one[0] = jnp.zeros(one.shape[1:], F32)
    lane = lax.shift_right_logical(
        lax.broadcasted_iota(jnp.int32, (NTGT, 128), 1), grp.bit_length() - 1
    )

    def held_body(held, carry):
        for slot in range(count):
            which, base = table_place(layout, slot, held)
            at = held * count + slot
            first_group = source_row(spread, slot, held) * per
            block = everyone[at]
            turned = quarter_turn(block)
            corr = lax.dot_general(targets[...], block, NT_DIMS, preferred_element_type=F32)
            results = []
            for low in range(0, per, duo):
                lanes = slice(low * grp, low * grp + span)
                lefts = []
                for one in range(duo):
                    pickup = jnp.where(lane == one, first_group + low + one, 127)
                    weight = jnp.take_along_axis(wanted[...], pickup, axis=1)[:, :span]
                    lefts.append(
                        jnp.concatenate(
                            [corr[:NTGT, lanes] * weight, corr[NTGT:, lanes] * weight], axis=1
                        ).astype(BF16)
                    )
                left = jnp.concatenate(
                    [part[t : t + tile] for t in range(0, NTGT, tile) for part in lefts], axis=0
                )
                both = jnp.concatenate([block[lanes], turned[lanes]], axis=0)
                results.append(jnp.dot(left, both, preferred_element_type=F32))
            for t in range(0, NTGT, tile):
                sums = [None]
                for part in range(per):
                    row = t * duo + (part % duo) * tile
                    one = results[part // duo][row : row + tile]
                    sums += [one] + [low + one for low in sums[1:]]
                for subset in range(1, len(sums)):
                    tables[which][base + subset, t : t + tile] = sums[subset]
        return carry

    lax.fori_loop(0, spread, held_body, 0)
    copy.wait()
    lefts = [blocks[slot * spread] for slot in slots]
    receive(layout, slots, tables, table, right, lefts, outs)


def rest_kernel(layout, slots, packed, first, second, *refs):
    lefts, refs = refs[: len(slots)], refs[len(slots) :]
    outs, (right, table, sem) = refs[: len(slots)], refs[len(slots) :]
    copy = pltpu.make_async_copy(packed, table, sem)
    copy.start()
    copy.wait()
    receive(layout, slots, (first, second), table, right, lefts, outs)


def near(value):
    return pltpu.with_memory_space_constraint(value, pltpu.VMEM)


def scratch(layout, slots, groups, width):
    _, _, own, _, grp = layout
    return [
        pltpu.VMEM((len(slots) * own // grp, 2 * NTGT, width), BF16),
        pltpu.SMEM((groups, 128), jnp.int32),
        pltpu.SemaphoreType.DMA,
    ]


def third(blocks, slots, packed, wanted, layout):
    count, spread, own, _, grp = layout
    width, per = blocks[0].shape[-1], own // grp
    return pl.pallas_call(
        functools.partial(third_kernel, layout, slots),
        in_specs=[VMEM] * (2 + count * spread),
        out_specs=[VMEM] * (2 + len(slots)),
        out_shape=[pltpu.VMEM(((count * spread // 2) << per, NTGT, width), F32)] * 2
        + [pltpu.VMEM((own, 2 * NTGT), BF16)] * len(slots),
        scratch_shapes=[
            pltpu.VMEM((count * spread, own, width), BF16),
            pltpu.VMEM((NTGT, width), F32),
            pltpu.VMEM((2 * NTGT, width), BF16),
        ]
        + scratch(layout, slots, packed.shape[0], width),
        compiler_params=pltpu.CompilerParams(vmem_limit_bytes=12 << 20),
        name="third",
    )(near(packed), near(wanted), *map(near, blocks))


def rest(lefts, slots, packed, tables, layout):
    own, width = lefts[0].shape
    return pl.pallas_call(
        functools.partial(rest_kernel, layout, slots),
        in_specs=[VMEM] * (3 + len(slots)),
        out_specs=[VMEM] * len(slots),
        out_shape=[pltpu.VMEM((own, 2 * NTGT), BF16)] * len(slots),
        scratch_shapes=scratch(layout, slots, packed.shape[0], width),
        compiler_params=pltpu.CompilerParams(vmem_limit_bytes=12 << 20),
        name="rest",
    )(near(packed), *map(near, tables), *map(near, lefts))


def finish_kernel(spread, *refs):
    blocks, out = refs[:-1], refs[-1]
    count = len(blocks)
    own = blocks[0].shape[0]
    mine = lax.axis_index("row") // spread
    for slot, block in enumerate(blocks):
        value = block[...].astype(F32)
        for part in range(2):
            out[pl.ds(part * count + (mine ^ slot), own, stride=2 * count), :] = value[
                :, part * NTGT : (part + 1) * NTGT
            ]


def finish(blocks, spread):
    own = blocks[0].shape[0]
    count = len(blocks)
    out = pl.pallas_call(
        functools.partial(finish_kernel, spread),
        in_specs=[VMEM] * count,
        out_specs=VMEM,
        out_shape=jax.ShapeDtypeStruct((own * 2 * count, NTGT), F32),
        name="finish",
    )(*map(near, blocks))
    return out.reshape(own, 2, count, NTGT)


def on_device(rows, spectra, coda_bins, source_mask):
    count = coda_bins.shape[0]
    spread = rows // count
    own = spectra.shape[2]
    channels = own * rows
    layout = (count, spread, own, channels // NTGT, channels // source_mask.shape[0])

    def swap(value, bits):
        return lax.ppermute(value, "row", [(r, r ^ bits) for r in range(rows)])

    *white, packed, wanted = whiten(spectra, coda_bins, source_mask, layout)
    blocks = [[white[0]] + [None] * (spread - 1)]
    for slot in range(1, count):
        blocks.append([swap(white[slot], slot * spread)] + [None] * (spread - 1))
    bit = spread // 2
    while bit >= 1:
        for slot in range(count):
            for held in range(0, spread, 2 * bit):
                blocks[slot][held + bit] = swap(blocks[slot][held], bit)
        bit //= 2
    flat = [blocks[slot][held] for slot in range(count) for held in range(spread)]
    stages = [(slot,) for slot in range(count // 2, count)] + [tuple(range(count // 2))]
    first, second, *parts = third(flat, stages[0], packed, wanted, layout)
    results = dict(zip(stages[0], parts))
    for stage in stages[1:]:
        lefts = [blocks[slot][0] for slot in stage]
        results.update(zip(stage, rest(lefts, stage, packed, (first, second), layout)))
    back = [results[0]] + [swap(results[slot], slot * spread) for slot in range(1, count)]
    return finish(back, spread)


def solution(mesh):
    def body(spectra, coda_bins, source_mask):
        return on_device(mesh.shape["row"], spectra, coda_bins, source_mask)

    return jax.shard_map(
        body,
        mesh=mesh,
        in_specs=(P(None, None, "row", "band"), P("band"), P("band", None)),
        out_specs=P(("band", "row"), None, None, None),
        check_vma=False,
    )
```

profile of v0, /device:TPU:0, one launch (start us, length us, event | category | flops | bytes accessed | tf_op | source)
XLA Modules:
  0.0 55.4 jit_solution(4931713597209201931)
XLA Ops:
  0.0 2.4 %whiten.1 = (bf16[256,256]{1,0:T(8,128)(2,1)S(1)}, bf16[256,256]{1,0:T(8,128)(2,1)S(1)}, bf16[256,256]{1,0:T(8,128)(2,1)S(1)}, bf16[256,256]{1,0:T(8,128)(2,1)S(...) custom-call(s32[4]{0:T(128)} %bins.1, f32[2,16,256,128]{3,2,1,0:T(8,128)} %spectra.1, s32[64,64]{1,0:T(8,128)} %mask.1), custom_call_target="tpu_custom_call" | custom-call | tf_op jit(solution)/shard_map/whiten/pallas_call | solution.py:60
  2.4 3.1 %collective-permute-start.3 = (bf16[256,256]{1,0:T(8,128)(2,1)S(1)}, bf16[256,256]{1,0:T(8,128)(2,1)S(1)}, u32[]{:S(2)}, u32[]{:S(2)}) collective-permute-start(bf16[256,256]{1,0:T(8,128)(2,1)S(1)} %get-tuple-element.19), channel_id=1, source_target_pairs={{0,4},{1,5},{2,6},{3,7},{4,0},{5,1},{6,2},{7,3},{8,12},{9,13},{10,... | collective-permute-start | bytes 393224 | tf_op jit(solution)/shard_map/ppermute | solution.py:278
  5.5 2.6 %collective-permute-start.7 = (bf16[256,256]{1,0:T(8,128)(2,1)S(1)}, bf16[256,256]{1,0:T(8,128)(2,1)S(1)}, u32[]{:S(2)}, u32[]{:S(2)}) collective-permute-start(bf16[256,256]{1,0:T(8,128)(2,1)S(1)} %get-tuple-element.20), channel_id=1, source_target_pairs={{0,8},{1,9},{2,10},{3,11},{4,12},{5,13},{6,14},{7,15},{8,0},{9,1},... | collective-permute-start | bytes 393224 | tf_op jit(solution)/shard_map/ppermute | solution.py:278
  8.1 0.0 collective-permute-start.11
  8.1 1.7 %collective-permute-start.1 = (bf16[256,256]{1,0:T(8,128)(2,1)S(1)}, bf16[256,256]{1,0:T(8,128)(2,1)S(1)}, u32[]{:S(2)}, u32[]{:S(2)}) collective-permute-start(bf16[256,256]{1,0:T(8,128)(2,1)S(1)} %get-tuple-element.18.refs_0_), channel_id=1, source_target_pairs={{0,2},{1,3},{2,0},{3,1},{4,6},{5,7},{6,4},{7,5},{8,10},{9,11},{10,... | collective-permute-start | bytes 393224 | tf_op jit(solution)/shard_map/ppermute | solution.py:278
  9.9 0.0 collective-permute-start
  9.9 0.7 %collective-permute-done.3.refs_4_.refs_1_ = bf16[256,256]{1,0:T(8,128)(2,1)S(1)} collective-permute-done((bf16[256,256]{1,0:T(8,128)(2,1)S(1)}, bf16[256,256]{1,0:T(8,128)(2,1)S(1)}, u32[]{:S(2)}, u32[]{:S(2)}) %collective-permute-start.3) | collective-permute-done | bytes 131104 | tf_op jit(solution)/shard_map/ppermute | solution.py:278
  10.6 1.7 %collective-permute-start.5 = (bf16[256,256]{1,0:T(8,128)(2,1)S(1)}, bf16[256,256]{1,0:T(8,128)(2,1)S(1)}, u32[]{:S(2)}, u32[]{:S(2)}) collective-permute-start(bf16[256,256]{1,0:T(8,128)(2,1)S(1)} %collective-permute-done.3.refs_4_.refs_1_), channel_id=1, source_target_pairs={{0,2},{1,3},{2,0},{3,1},{4,6},{5,7},{6,4},{7,5},{8,10},{9,11},{10,... | collective-permute-start | bytes 393224 | tf_op jit(solution)/shard_map/ppermute | solution.py:278
  12.3 6.1 %collective-permute-done.7.refs_8_ = bf16[256,256]{1,0:T(8,128)(2,1)S(1)} collective-permute-done((bf16[256,256]{1,0:T(8,128)(2,1)S(1)}, bf16[256,256]{1,0:T(8,128)(2,1)S(1)}, u32[]{:S(2)}, u32[]{:S(2)}) %collective-permute-start.7) | collective-permute-done | bytes 131104 | tf_op jit(solution)/shard_map/ppermute | solution.py:278
  18.4 0.0 collective-permute-start.4
  18.4 0.0 collective-permute-done.11.refs_12_.refs_0_
  18.4 1.5 %collective-permute-start.9 = (bf16[256,256]{1,0:T(8,128)(2,1)S(1)}, bf16[256,256]{1,0:T(8,128)(2,1)S(1)}, u32[]{:S(2)}, u32[]{:S(2)}) collective-permute-start(bf16[256,256]{1,0:T(8,128)(2,1)S(1)} %collective-permute-done.7.refs_8_), channel_id=1, source_target_pairs={{0,2},{1,3},{2,0},{3,1},{4,6},{5,7},{6,4},{7,5},{8,10},{9,11},{10,... | collective-permute-start | bytes 393224 | tf_op jit(solution)/shard_map/ppermute | solution.py:278
  19.9 0.0 collective-permute-done.1.refs_2_
  19.9 0.2 collective-permute-start.8
  20.2 0.0 collective-permute-done.refs_1_
  20.2 0.5 collective-permute-start.13
  20.7 0.0 collective-permute-done.5.refs_6_
  20.7 0.0 collective-permute-start.12
  20.7 0.0 collective-permute-done.4.refs_5_
  20.7 0.5 collective-permute-start.2
  21.2 3.6 %collective-permute-done.9.refs_10_ = bf16[256,256]{1,0:T(8,128)(2,1)S(1)} collective-permute-done((bf16[256,256]{1,0:T(8,128)(2,1)S(1)}, bf16[256,256]{1,0:T(8,128)(2,1)S(1)}, u32[]{:S(2)}, u32[]{:S(2)}) %collective-permute-start.9) | collective-permute-done | bytes 131104 | tf_op jit(solution)/shard_map/ppermute | solution.py:278
  24.8 0.0 collective-permute-start.6
  24.8 0.0 collective-permute-done.8.refs_9_
  24.8 0.5 collective-permute-start.10
  25.3 1.8 %collective-permute-done.13.refs_14_ = bf16[256,256]{1,0:T(8,128)(2,1)S(1)} collective-permute-done((bf16[256,256]{1,0:T(8,128)(2,1)S(1)}, bf16[256,256]{1,0:T(8,128)(2,1)S(1)}, u32[]{:S(2)}, u32[]{:S(2)}) %collective-permute-start.13) | collective-permute-done | bytes 131104 | tf_op jit(solution)/shard_map/ppermute | solution.py:278
  27.1 0.0 collective-permute-start.14
  27.1 0.0 collective-permute-done.12.refs_13_
  27.1 0.0 collective-permute-done.2.refs_3_
  27.1 0.0 collective-permute-done.6.refs_7_
  27.2 0.0 collective-permute-done.10.refs_11_
  27.2 1.3 %collective-permute-done.14.refs_15_ = bf16[256,256]{1,0:T(8,128)(2,1)S(1)} collective-permute-done((bf16[256,256]{1,0:T(8,128)(2,1)S(1)}, bf16[256,256]{1,0:T(8,128)(2,1)S(1)}, u32[]{:S(2)}, u32[]{:S(2)}) %collective-permute-start.14) | collective-permute-done | bytes 131104 | tf_op jit(solution)/shard_map/ppermute | solution.py:278
  28.5 6.0 %third.1 = (f32[128,128,256]{2,1,0:T(8,128)S(1)}, f32[128,128,256]{2,1,0:T(8,128)S(1)}, bf16[256,256]{1,0:T(8,128)(2,1)S(1)}) custom-call(s32[64,128]{1,0:T(8,128)S(1)} %get-tuple-element.16.packed, f32[128,128]{1,0:T(8,128)S(1)} %get-tuple-element.17.wanted, bf16[256,256]{1,0:T(8,128)(2,1)S(1)} %get-tuple-element.18.refs_0_, ...), custom_call_target="tpu_custom_call" | custom-call | tf_op jit(solution)/shard_map/third/pallas_call | solution.py:214
  34.5 2.5 %rest.2 = (bf16[256,256]{1,0:T(8,128)(2,1)S(1)}, bf16[256,256]{1,0:T(8,128)(2,1)S(1)}) custom-call(s32[64,128]{1,0:T(8,128)S(1)} %get-tuple-element.16.packed, f32[128,128,256]{2,1,0:T(8,128)S(1)} %get-tuple-element.22.first, f32[128,128,256]{2,1,0:T(8,128)S(1)} %get-tuple-element.23.second, bf16[256,256]{1,0:T(8,128)(2,1)S(1)} %get-tuple-element.18.refs_0_, ...), custom_call_target="tpu_custom_call" | custom-call | tf_op jit(solution)/shard_map/rest/pallas_call | solution.py:233
  37.0 1.1 %collective-permute-start.15 = (bf16[256,256]{1,0:T(8,128)(2,1)S(1)}, bf16[256,256]{1,0:T(8,128)(2,1)S(1)}, u32[]{:S(2)}, u32[]{:S(2)}) collective-permute-start(bf16[256,256]{1,0:T(8,128)(2,1)S(1)} %get-tuple-element.25), channel_id=1, source_target_pairs={{0,4},{1,5},{2,6},{3,7},{4,0},{5,1},{6,2},{7,3},{8,12},{9,13},{10,... | collective-permute-start | bytes 393224 | tf_op jit(solution)/shard_map/ppermute | solution.py:278
  38.2 1.9 %rest.3 = bf16[256,256]{1,0:T(8,128)(2,1)S(1)} custom-call(s32[64,128]{1,0:T(8,128)S(1)} %get-tuple-element.16.packed, f32[128,128,256]{2,1,0:T(8,128)S(1)} %get-tuple-element.22.first, f32[128,128,256]{2,1,0:T(8,128)S(1)} %get-tuple-element.23.second, bf16[256,256]{1,0:T(8,128)(2,1)S(1)} %collective-permute-done.11.refs_12_.refs_0_), custom_call_target="tpu_custom_call" | custom-call | tf_op jit(solution)/shard_map/rest/pallas_call | solution.py:233
  40.0 2.5 %collective-permute-start.17 = (bf16[256,256]{1,0:T(8,128)(2,1)S(1)}, bf16[256,256]{1,0:T(8,128)(2,1)S(1)}, u32[]{:S(2)}, u32[]{:S(2)}) collective-permute-start(bf16[256,256]{1,0:T(8,128)(2,1)S(1)} %rest.3), channel_id=1, source_target_pairs={{0,12},{1,13},{2,14},{3,15},{4,8},{5,9},{6,10},{7,11},{8,4},{9,5},... | collective-permute-start | bytes 393224 | tf_op jit(solution)/shard_map/ppermute | solution.py:278
  42.6 0.0 collective-permute-start.16
  42.6 0.1 collective-permute-done.15.refs_1_
  42.6 5.7 %collective-permute-done.17.refs_3_ = bf16[256,256]{1,0:T(8,128)(2,1)S(1)} collective-permute-done((bf16[256,256]{1,0:T(8,128)(2,1)S(1)}, bf16[256,256]{1,0:T(8,128)(2,1)S(1)}, u32[]{:S(2)}, u32[]{:S(2)}) %collective-permute-start.17) | collective-permute-done | bytes 131104 | tf_op jit(solution)/shard_map/ppermute | solution.py:278
  48.3 5.9 %collective-permute-done.16.refs_2_ = bf16[256,256]{1,0:T(8,128)(2,1)S(1)} collective-permute-done((bf16[256,256]{1,0:T(8,128)(2,1)S(1)}, bf16[256,256]{1,0:T(8,128)(2,1)S(1)}, u32[]{:S(2)}, u32[]{:S(2)}) %collective-permute-start.16) | collective-permute-done | bytes 131104 | tf_op jit(solution)/shard_map/ppermute | solution.py:278
  54.2 1.2 %finish.1 = f32[2048,128]{1,0:T(8,128)} custom-call(bf16[256,256]{1,0:T(8,128)(2,1)S(1)} %get-tuple-element.24.refs_0_, bf16[256,256]{1,0:T(8,128)(2,1)S(1)} %collective-permute-done.15.refs_1_, bf16[256,256]{1,0:T(8,128)(2,1)S(1)} %collective-permute-done.16.refs_2_, bf16[256,256]{1,0:T(8,128)(2,1)S(1)} %collective-permute-done.17.refs_3_), custom_call_target="tpu_custom_call" | custom-call | tf_op jit(solution)/shard_map/finish/pallas_call | solution.py:260
Async XLA Ops:
  2.4 8.2 %collective-permute-start.3 = (bf16[256,256]{1,0:T(8,128)(2,1)S(1)}, bf16[256,256]{1,0:T(8,128)(2,1)S(1)}, u32[]{:S(2)}, u32[]{:S(2)}) collective-permute-start(bf16[256,256]{1,0:T(8,128)(2,1)S(1)} %get-tuple-element.19), channel_id=1, source_target_pairs={{0,4},{1,5},{2,6},{3,7},{4,0},{5,1},{6,2},{7,3},{8,12},{9,13},{10,... | collective-permute-start | bytes 393224 | tf_op jit(solution)/shard_map/ppermute | solution.py:278
  5.5 12.9 %collective-permute-start.7 = (bf16[256,256]{1,0:T(8,128)(2,1)S(1)}, bf16[256,256]{1,0:T(8,128)(2,1)S(1)}, u32[]{:S(2)}, u32[]{:S(2)}) collective-permute-start(bf16[256,256]{1,0:T(8,128)(2,1)S(1)} %get-tuple-element.20), channel_id=1, source_target_pairs={{0,8},{1,9},{2,10},{3,11},{4,12},{5,13},{6,14},{7,15},{8,0},{9,1},... | collective-permute-start | bytes 393224 | tf_op jit(solution)/shard_map/ppermute | solution.py:278
  8.1 10.3 %collective-permute-start.11 = (bf16[256,256]{1,0:T(8,128)(2,1)S(1)}, bf16[256,256]{1,0:T(8,128)(2,1)S(1)}, u32[]{:S(2)}, u32[]{:S(2)}) collective-permute-start(bf16[256,256]{1,0:T(8,128)(2,1)S(1)} %get-tuple-element.21), channel_id=1, source_target_pairs={{0,12},{1,13},{2,14},{3,15},{4,8},{5,9},{6,10},{7,11},{8,4},{9,5},... | collective-permute-start | bytes 393224 | tf_op jit(solution)/shard_map/ppermute | solution.py:278
  8.1 11.8 %collective-permute-start.1 = (bf16[256,256]{1,0:T(8,128)(2,1)S(1)}, bf16[256,256]{1,0:T(8,128)(2,1)S(1)}, u32[]{:S(2)}, u32[]{:S(2)}) collective-permute-start(bf16[256,256]{1,0:T(8,128)(2,1)S(1)} %get-tuple-element.18.refs_0_), channel_id=1, source_target_pairs={{0,2},{1,3},{2,0},{3,1},{4,6},{5,7},{6,4},{7,5},{8,10},{9,11},{10,... | collective-permute-start | bytes 393224 | tf_op jit(solution)/shard_map/ppermute | solution.py:278
  9.9 10.3 %collective-permute-start = (bf16[256,256]{1,0:T(8,128)(2,1)S(1)}, bf16[256,256]{1,0:T(8,128)(2,1)S(1)}, u32[]{:S(2)}, u32[]{:S(2)}) collective-permute-start(bf16[256,256]{1,0:T(8,128)(2,1)S(1)} %get-tuple-element.18.refs_0_), channel_id=1, source_target_pairs={{0,1},{1,0},{2,3},{3,2},{4,5},{5,4},{6,7},{7,6},{8,9},{9,8},{10,11... | collective-permute-start | bytes 393224 | tf_op jit(solution)/shard_map/ppermute | solution.py:278
  10.6 10.1 %collective-permute-start.5 = (bf16[256,256]{1,0:T(8,128)(2,1)S(1)}, bf16[256,256]{1,0:T(8,128)(2,1)S(1)}, u32[]{:S(2)}, u32[]{:S(2)}) collective-permute-start(bf16[256,256]{1,0:T(8,128)(2,1)S(1)} %collective-permute-done.3.refs_4_.refs_1_), channel_id=1, source_target_pairs={{0,2},{1,3},{2,0},{3,1},{4,6},{5,7},{6,4},{7,5},{8,10},{9,11},{10,... | collective-permute-start | bytes 393224 | tf_op jit(solution)/shard_map/ppermute | solution.py:278
  18.4 2.3 %collective-permute-start.4 = (bf16[256,256]{1,0:T(8,128)(2,1)S(1)}, bf16[256,256]{1,0:T(8,128)(2,1)S(1)}, u32[]{:S(2)}, u32[]{:S(2)}) collective-permute-start(bf16[256,256]{1,0:T(8,128)(2,1)S(1)} %collective-permute-done.3.refs_4_.refs_1_), channel_id=1, source_target_pairs={{0,1},{1,0},{2,3},{3,2},{4,5},{5,4},{6,7},{7,6},{8,9},{9,8},{10,11... | collective-permute-start | bytes 393224 | tf_op jit(solution)/shard_map/ppermute | solution.py:278
  18.4 6.4 %collective-permute-start.9 = (bf16[256,256]{1,0:T(8,128)(2,1)S(1)}, bf16[256,256]{1,0:T(8,128)(2,1)S(1)}, u32[]{:S(2)}, u32[]{:S(2)}) collective-permute-start(bf16[256,256]{1,0:T(8,128)(2,1)S(1)} %collective-permute-done.7.refs_8_), channel_id=1, source_target_pairs={{0,2},{1,3},{2,0},{3,1},{4,6},{5,7},{6,4},{7,5},{8,10},{9,11},{10,... | collective-permute-start | bytes 393224 | tf_op jit(solution)/shard_map/ppermute | solution.py:278
  19.9 4.9 %collective-permute-start.8 = (bf16[256,256]{1,0:T(8,128)(2,1)S(1)}, bf16[256,256]{1,0:T(8,128)(2,1)S(1)}, u32[]{:S(2)}, u32[]{:S(2)}) collective-permute-start(bf16[256,256]{1,0:T(8,128)(2,1)S(1)} %collective-permute-done.7.refs_8_), channel_id=1, source_target_pairs={{0,1},{1,0},{2,3},{3,2},{4,5},{5,4},{6,7},{7,6},{8,9},{9,8},{10,11... | collective-permute-start | bytes 393224 | tf_op jit(solution)/shard_map/ppermute | solution.py:278
  20.2 7.0 %collective-permute-start.13 = (bf16[256,256]{1,0:T(8,128)(2,1)S(1)}, bf16[256,256]{1,0:T(8,128)(2,1)S(1)}, u32[]{:S(2)}, u32[]{:S(2)}) collective-permute-start(bf16[256,256]{1,0:T(8,128)(2,1)S(1)} %collective-permute-done.11.refs_12_.refs_0_), channel_id=1, source_target_pairs={{0,2},{1,3},{2,0},{3,1},{4,6},{5,7},{6,4},{7,5},{8,10},{9,11},{10,... | collective-permute-start | bytes 393224 | tf_op jit(solution)/shard_map/ppermute | solution.py:278
  20.7 6.5 %collective-permute-start.12 = (bf16[256,256]{1,0:T(8,128)(2,1)S(1)}, bf16[256,256]{1,0:T(8,128)(2,1)S(1)}, u32[]{:S(2)}, u32[]{:S(2)}) collective-permute-start(bf16[256,256]{1,0:T(8,128)(2,1)S(1)} %collective-permute-done.11.refs_12_.refs_0_), channel_id=1, source_target_pairs={{0,1},{1,0},{2,3},{3,2},{4,5},{5,4},{6,7},{7,6},{8,9},{9,8},{10,11... | collective-permute-start | bytes 393224 | tf_op jit(solution)/shard_map/ppermute | solution.py:278
  20.7 6.5 %collective-permute-start.2 = (bf16[256,256]{1,0:T(8,128)(2,1)S(1)}, bf16[256,256]{1,0:T(8,128)(2,1)S(1)}, u32[]{:S(2)}, u32[]{:S(2)}) collective-permute-start(bf16[256,256]{1,0:T(8,128)(2,1)S(1)} %collective-permute-done.1.refs_2_), channel_id=1, source_target_pairs={{0,1},{1,0},{2,3},{3,2},{4,5},{5,4},{6,7},{7,6},{8,9},{9,8},{10,11... | collective-permute-start | bytes 393224 | tf_op jit(solution)/shard_map/ppermute | solution.py:278
  24.8 2.4 %collective-permute-start.6 = (bf16[256,256]{1,0:T(8,128)(2,1)S(1)}, bf16[256,256]{1,0:T(8,128)(2,1)S(1)}, u32[]{:S(2)}, u32[]{:S(2)}) collective-permute-start(bf16[256,256]{1,0:T(8,128)(2,1)S(1)} %collective-permute-done.5.refs_6_), channel_id=1, source_target_pairs={{0,1},{1,0},{2,3},{3,2},{4,5},{5,4},{6,7},{7,6},{8,9},{9,8},{10,11... | collective-permute-start | bytes 393224 | tf_op jit(solution)/shard_map/ppermute | solution.py:278
  24.8 2.4 %collective-permute-start.10 = (bf16[256,256]{1,0:T(8,128)(2,1)S(1)}, bf16[256,256]{1,0:T(8,128)(2,1)S(1)}, u32[]{:S(2)}, u32[]{:S(2)}) collective-permute-start(bf16[256,256]{1,0:T(8,128)(2,1)S(1)} %collective-permute-done.9.refs_10_), channel_id=1, source_target_pairs={{0,1},{1,0},{2,3},{3,2},{4,5},{5,4},{6,7},{7,6},{8,9},{9,8},{10,11... | collective-permute-start | bytes 393224 | tf_op jit(solution)/shard_map/ppermute | solution.py:278
  27.1 1.3 %collective-permute-start.14 = (bf16[256,256]{1,0:T(8,128)(2,1)S(1)}, bf16[256,256]{1,0:T(8,128)(2,1)S(1)}, u32[]{:S(2)}, u32[]{:S(2)}) collective-permute-start(bf16[256,256]{1,0:T(8,128)(2,1)S(1)} %collective-permute-done.13.refs_14_), channel_id=1, source_target_pairs={{0,1},{1,0},{2,3},{3,2},{4,5},{5,4},{6,7},{7,6},{8,9},{9,8},{10,11... | collective-permute-start | bytes 393224 | tf_op jit(solution)/shard_map/ppermute | solution.py:278
  37.0 5.6 %collective-permute-start.15 = (bf16[256,256]{1,0:T(8,128)(2,1)S(1)}, bf16[256,256]{1,0:T(8,128)(2,1)S(1)}, u32[]{:S(2)}, u32[]{:S(2)}) collective-permute-start(bf16[256,256]{1,0:T(8,128)(2,1)S(1)} %get-tuple-element.25), channel_id=1, source_target_pairs={{0,4},{1,5},{2,6},{3,7},{4,0},{5,1},{6,2},{7,3},{8,12},{9,13},{10,... | collective-permute-start | bytes 393224 | tf_op jit(solution)/shard_map/ppermute | solution.py:278
  40.0 8.3 %collective-permute-start.17 = (bf16[256,256]{1,0:T(8,128)(2,1)S(1)}, bf16[256,256]{1,0:T(8,128)(2,1)S(1)}, u32[]{:S(2)}, u32[]{:S(2)}) collective-permute-start(bf16[256,256]{1,0:T(8,128)(2,1)S(1)} %rest.3), channel_id=1, source_target_pairs={{0,12},{1,13},{2,14},{3,15},{4,8},{5,9},{6,10},{7,11},{8,4},{9,5},... | collective-permute-start | bytes 393224 | tf_op jit(solution)/shard_map/ppermute | solution.py:278
  42.6 11.6 %collective-permute-start.16 = (bf16[256,256]{1,0:T(8,128)(2,1)S(1)}, bf16[256,256]{1,0:T(8,128)(2,1)S(1)}, u32[]{:S(2)}, u32[]{:S(2)}) collective-permute-start(bf16[256,256]{1,0:T(8,128)(2,1)S(1)} %get-tuple-element.26), channel_id=1, source_target_pairs={{0,8},{1,9},{2,10},{3,11},{4,12},{5,13},{6,14},{7,15},{8,0},{9,1},... | collective-permute-start | bytes 393224 | tf_op jit(solution)/shard_map/ppermute | solution.py:278
where the time goes:
time: 55.6 us; the launch traced here: 55.4 us
  waiting for transfers between devices  25.2 us (45%)
  starting transfers between devices  16.1 us (29%)
  Pallas kernels  14 us (25%)
    ppermute x18, waiting for transfers between devices, swap(): return lax.ppermute(value, 'row', [(r, r ^ bits) for r in range(rows)])  25.2 us
    ppermute x18, starting transfers between devices, swap(): return lax.ppermute(value, 'row', [(r, r ^ bits) for r in range(rows)])  16.1 us
    pallas_call x1, Pallas kernels, third(): pl.pallas_call(functools.partial(third_kernel, layout, slots), in_specs=[...  6.02 us
    pallas_call x2, Pallas kernels, rest(): pl.pallas_call(functools.partial(rest_kernel, layout, slots), in_specs=[V...  4.36 us
    pallas_call x1, Pallas kernels, whiten(): pl.pallas_call(functools.partial(whiten_kernel, layout), in_specs=[SMEM,...  2.4 us
    pallas_call x1, Pallas kernels, finish(): pl.pallas_call(functools.partial(finish_kernel, spread), in_specs=[VMEM]...  1.25 us
  transfers between devices with their start and end apart: 18, of which 8 were waited for; matrix products, arithmetic and copies ran while one was open for 0% of the time, Pallas kernels for 3%

commit v1 on v0

--- a/solution.py
+++ b/solution.py
@@ -33,41 +33,46 @@
     wanted[...] = jnp.dot(rowpick, values, preferred_element_type=F32)
 
 
-def whiten_kernel(layout, bins, spectra, mask, *refs):
-    count, spread = layout[:2]
-    outs, (packed, wanted, held, sems, near_mask, mask_sem) = refs[:count], refs[count:]
+def whiten_kernel(layout, slots, bins, spectra, mask, *refs):
+    spread, final = layout[1], 0 in slots
+    outs, refs = refs[: len(slots)], refs[len(slots) :]
+    if final:
+        packed, wanted, near_mask, mask_sem, *refs = refs
+    held, sems = refs
     mine = lax.axis_index("row") // spread
-    fetch = pltpu.make_async_copy(mask, near_mask, mask_sem)
     copies = [
-        pltpu.make_async_copy(spectra.at[:, bins[mine ^ slot]], held.at[slot], sems.at[slot])
-        for slot in range(count)
+        pltpu.make_async_copy(spectra.at[:, bins[mine ^ slot]], held.at[at], sems.at[at])
+        for at, slot in enumerate(slots)
     ]
-    for copy in (*copies, fetch):
+    if final:
+        copies.append(pltpu.make_async_copy(mask, near_mask, mask_sem))
+    for copy in copies:
         copy.start()
-    for slot in range(count):
-        copies[slot].wait()
-        real, imag = held[slot, 0], held[slot, 1]
+    for at in range(len(slots)):
+        copies[at].wait()
+        real, imag = held[at, 0], held[at, 1]
         power = jnp.mean(real * real + imag * imag, axis=1, keepdims=True)
         scale = 1.0 / jnp.sqrt(power + 1e-06)
-        outs[slot][...] = jnp.concatenate([real * scale, imag * scale], axis=1).astype(BF16)
-    fetch.wait()
-    ready(layout, near_mask, packed, wanted)
-
-
-def whiten(spectra, bins, mask, layout):
+        outs[at][...] = jnp.concatenate([real * scale, imag * scale], axis=1).astype(BF16)
+    if final:
+        copies[-1].wait()
+        ready(layout, near_mask, packed, wanted)
+
+
+def whiten(spectra, bins, mask, slots, layout):
     _, _, own, windows = spectra.shape
-    count = bins.shape[0]
+    final = 0 in slots
+    tables = [pltpu.VMEM((mask.shape[0], 128), jnp.int32), pltpu.VMEM((NTGT, 128), F32)]
+    fetched = [pltpu.VMEM(mask.shape, jnp.int32), pltpu.SemaphoreType.DMA]
     return pl.pallas_call(
-        functools.partial(whiten_kernel, layout),
+        functools.partial(whiten_kernel, layout, slots),
         in_specs=[SMEM, ANY, ANY],
-        out_specs=[VMEM] * (count + 2),
-        out_shape=[pltpu.VMEM((own, 2 * windows), BF16)] * count
-        + [pltpu.VMEM((mask.shape[0], 128), jnp.int32), pltpu.VMEM((NTGT, 128), F32)],
-        scratch_shapes=[
-            pltpu.VMEM((count, 2, own, windows), F32),
-            pltpu.SemaphoreType.DMA((count,)),
-            pltpu.VMEM(mask.shape, jnp.int32),
-            pltpu.SemaphoreType.DMA,
+        out_specs=[VMEM] * (len(slots) + 2 * final),
+        out_shape=[pltpu.VMEM((own, 2 * windows), BF16)] * len(slots) + tables * final,
+        scratch_shapes=fetched * final
+        + [
+            pltpu.VMEM((len(slots), 2, own, windows), F32),
+            pltpu.SemaphoreType.DMA((len(slots),)),
         ],
         name="whiten",
     )(bins, spectra, mask)
@@ -277,7 +282,11 @@
     def swap(value, bits):
         return lax.ppermute(value, "row", [(r, r ^ bits) for r in range(rows)])
 
-    *white, packed, wanted = whiten(spectra, coda_bins, source_mask, layout)
+    first_slots = (1, 2)
+    other = tuple(slot for slot in range(count) if slot not in first_slots)
+    white = dict(zip(first_slots, whiten(spectra, coda_bins, source_mask, first_slots, layout)))
+    *more, packed, wanted = whiten(spectra, coda_bins, source_mask, other, layout)
+    white.update(zip(other, more))
     blocks = [[white[0]] + [None] * (spread - 1)]
     for slot in range(1, count):
         blocks.append([swap(white[slot], slot * spread)] + [None] * (spread - 1))

time: 55.6 us -> 54.8 us (0.986)
  waiting for transfers between devices: 25.2 us -> 22.7 us
  Pallas kernels: 14 us -> 15.7 us
    ppermute x18, waiting for transfers between devices: 25.2 us -> 22.7 us  [swap(): return lax.ppermute(value, 'row', [(r, r ^ bits) for r in range(rows)])]
    pallas_call x1 -> x2, Pallas kernels: 2.4 us -> 4.02 us  [whiten(): pl.pallas_call(functools.partial(whiten_kernel, layout, slots), in_specs=...]
  transfers between devices with their start and end apart: 18 -> 18, of which waited for: 8 -> 6; matrix products, arithmetic and copies ran while one was open for 0% -> 0% of each run, Pallas kernels for 3% -> 7%
where the time goes in v1:
time: 54.8 us; the launch traced here: 54.6 us
  waiting for transfers between devices  22.7 us (41%)
  starting transfers between devices  16.2 us (30%)
  Pallas kernels  15.7 us (29%)
    ppermute x18, waiting for transfers between devices, swap(): return lax.ppermute(value, 'row', [(r, r ^ bits) for r in range(rows)])  22.7 us
    ppermute x18, starting transfers between devices, swap(): return lax.ppermute(value, 'row', [(r, r ^ bits) for r in range(rows)])  16.2 us
    pallas_call x1, Pallas kernels, third(): pl.pallas_call(functools.partial(third_kernel, layout, slots), in_specs=[...  6.02 us
    pallas_call x2, Pallas kernels, rest(): pl.pallas_call(functools.partial(rest_kernel, layout, slots), in_specs=[V...  4.36 us
    pallas_call x2, Pallas kernels, whiten(): pl.pallas_call(functools.partial(whiten_kernel, layout, slots), in_specs=...  4.02 us
    pallas_call x1, Pallas kernels, finish(): pl.pallas_call(functools.partial(finish_kernel, spread), in_specs=[VMEM]...  1.25 us
  transfers between devices with their start and end apart: 18, of which 6 were waited for; matrix products, arithmetic and copies ran while one was open for 0% of the time, Pallas kernels for 7%

profile of v1, /device:TPU:0, one launch (start us, length us, event | category | flops | bytes accessed | tf_op | source)
XLA Modules:
  0.0 54.6 jit_solution(14468604956129265337)
XLA Ops:
  0.0 1.9 %whiten.3 = (bf16[256,256]{1,0:T(8,128)(2,1)S(1)}, bf16[256,256]{1,0:T(8,128)(2,1)S(1)}) custom-call(s32[4]{0:T(128)} %bins.3, f32[2,16,256,128]{3,2,1,0:T(8,128)} %spectra.3, s32[64,64]{1,0:T(8,128)} %mask.3), custom_call_target="tpu_custom_call" | custom-call | tf_op jit(solution)/shard_map/whiten/pallas_call | solution.py:67
  1.9 3.1 %collective-permute-start.3 = (bf16[256,256]{1,0:T(8,128)(2,1)S(1)}, bf16[256,256]{1,0:T(8,128)(2,1)S(1)}, u32[]{:S(2)}, u32[]{:S(2)}) collective-permute-start(bf16[256,256]{1,0:T(8,128)(2,1)S(1)} %get-tuple-element.19), channel_id=1, source_target_pairs={{0,4},{1,5},{2,6},{3,7},{4,0},{5,1},{6,2},{7,3},{8,12},{9,13},{10,... | collective-permute-start | bytes 393224 | tf_op jit(solution)/shard_map/ppermute | solution.py:283
  5.1 2.6 %collective-permute-start.7 = (bf16[256,256]{1,0:T(8,128)(2,1)S(1)}, bf16[256,256]{1,0:T(8,128)(2,1)S(1)}, u32[]{:S(2)}, u32[]{:S(2)}) collective-permute-start(bf16[256,256]{1,0:T(8,128)(2,1)S(1)} %get-tuple-element.20), channel_id=1, source_target_pairs={{0,8},{1,9},{2,10},{3,11},{4,12},{5,13},{6,14},{7,15},{8,0},{9,1},... | collective-permute-start | bytes 393224 | tf_op jit(solution)/shard_map/ppermute | solution.py:283
  7.7 2.1 %whiten.2 = (bf16[256,256]{1,0:T(8,128)(2,1)S(1)}, bf16[256,256]{1,0:T(8,128)(2,1)S(1)}, s32[64,128]{1,0:T(8,128)S(1)}, f32[128,128]{1,0:T(8,128)S(1)}) custom-call(s32[4]{0:T(128)} %bins.3, f32[2,16,256,128]{3,2,1,0:T(8,128)} %spectra.3, s32[64,64]{1,0:T(8,128)} %mask.3), custom_call_target="tpu_custom_call" | custom-call | tf_op jit(solution)/shard_map/whiten/pallas_call | solution.py:67
  9.7 0.1 collective-permute-start.11
  9.8 1.7 %collective-permute-start.1 = (bf16[256,256]{1,0:T(8,128)(2,1)S(1)}, bf16[256,256]{1,0:T(8,128)(2,1)S(1)}, u32[]{:S(2)}, u32[]{:S(2)}) collective-permute-start(bf16[256,256]{1,0:T(8,128)(2,1)S(1)} %get-tuple-element.18.refs_0_), channel_id=1, source_target_pairs={{0,2},{1,3},{2,0},{3,1},{4,6},{5,7},{6,4},{7,5},{8,10},{9,11},{10,... | collective-permute-start | bytes 393224 | tf_op jit(solution)/shard_map/ppermute | solution.py:283
  11.6 0.0 collective-permute-start
  11.6 0.0 collective-permute-done.3.refs_4_.refs_1_
  11.6 0.7 %collective-permute-start.5 = (bf16[256,256]{1,0:T(8,128)(2,1)S(1)}, bf16[256,256]{1,0:T(8,128)(2,1)S(1)}, u32[]{:S(2)}, u32[]{:S(2)}) collective-permute-start(bf16[256,256]{1,0:T(8,128)(2,1)S(1)} %collective-permute-done.3.refs_4_.refs_1_), channel_id=1, source_target_pairs={{0,2},{1,3},{2,0},{3,1},{4,6},{5,7},{6,4},{7,5},{8,10},{9,11},{10,... | collective-permute-start | bytes 393224 | tf_op jit(solution)/shard_map/ppermute | solution.py:283
  12.3 4.7 %collective-permute-done.7.refs_8_ = bf16[256,256]{1,0:T(8,128)(2,1)S(1)} collective-permute-done((bf16[256,256]{1,0:T(8,128)(2,1)S(1)}, bf16[256,256]{1,0:T(8,128)(2,1)S(1)}, u32[]{:S(2)}, u32[]{:S(2)}) %collective-permute-start.7) | collective-permute-done | bytes 131104 | tf_op jit(solution)/shard_map/ppermute | solution.py:283
  17.0 0.0 collective-permute-start.4
  17.0 0.0 collective-permute-done.11.refs_12_.refs_0_
  17.0 1.5 %collective-permute-start.9 = (bf16[256,256]{1,0:T(8,128)(2,1)S(1)}, bf16[256,256]{1,0:T(8,128)(2,1)S(1)}, u32[]{:S(2)}, u32[]{:S(2)}) collective-permute-start(bf16[256,256]{1,0:T(8,128)(2,1)S(1)} %collective-permute-done.7.refs_8_), channel_id=1, source_target_pairs={{0,2},{1,3},{2,0},{3,1},{4,6},{5,7},{6,4},{7,5},{8,10},{9,11},{10,... | collective-permute-start | bytes 393224 | tf_op jit(solution)/shard_map/ppermute | solution.py:283
  18.5 0.0 collective-permute-done.1.refs_2_
  18.5 0.2 collective-permute-start.8
  18.7 0.0 collective-permute-done.refs_1_
  18.7 0.5 collective-permute-start.13
  19.2 0.0 collective-permute-done.5.refs_6_
  19.2 0.0 collective-permute-start.12
  19.2 0.0 collective-permute-done.4.refs_5_
  19.2 0.5 collective-permute-start.2
  19.7 3.6 %collective-permute-done.9.refs_10_ = bf16[256,256]{1,0:T(8,128)(2,1)S(1)} collective-permute-done((bf16[256,256]{1,0:T(8,128)(2,1)S(1)}, bf16[256,256]{1,0:T(8,128)(2,1)S(1)}, u32[]{:S(2)}, u32[]{:S(2)}) %collective-permute-start.9) | collective-permute-done | bytes 131104 | tf_op jit(solution)/shard_map/ppermute | solution.py:283
  23.3 0.0 collective-permute-start.6
  23.3 0.0 collective-permute-done.8.refs_9_
  23.3 0.5 collective-permute-start.10
  23.8 1.8 %collective-permute-done.13.refs_14_ = bf16[256,256]{1,0:T(8,128)(2,1)S(1)} collective-permute-done((bf16[256,256]{1,0:T(8,128)(2,1)S(1)}, bf16[256,256]{1,0:T(8,128)(2,1)S(1)}, u32[]{:S(2)}, u32[]{:S(2)}) %collective-permute-start.13) | collective-permute-done | bytes 131104 | tf_op jit(solution)/shard_map/ppermute | solution.py:283
  25.7 0.0 collective-permute-start.14
  25.7 0.0 collective-permute-done.12.refs_13_
  25.7 0.0 collective-permute-done.2.refs_3_
  25.7 0.0 collective-permute-done.6.refs_7_
  25.7 0.0 collective-permute-done.10.refs_11_
  25.7 1.3 %collective-permute-done.14.refs_15_ = bf16[256,256]{1,0:T(8,128)(2,1)S(1)} collective-permute-done((bf16[256,256]{1,0:T(8,128)(2,1)S(1)}, bf16[256,256]{1,0:T(8,128)(2,1)S(1)}, u32[]{:S(2)}, u32[]{:S(2)}) %collective-permute-start.14) | collective-permute-done | bytes 131104 | tf_op jit(solution)/shard_map/ppermute | solution.py:283
  27.0 6.0 %third.1 = (f32[128,128,256]{2,1,0:T(8,128)S(1)}, f32[128,128,256]{2,1,0:T(8,128)S(1)}, bf16[256,256]{1,0:T(8,128)(2,1)S(1)}) custom-call(s32[64,128]{1,0:T(8,128)S(1)} %get-tuple-element.16.packed, f32[128,128]{1,0:T(8,128)S(1)} %get-tuple-element.17.wanted, bf16[256,256]{1,0:T(8,128)(2,1)S(1)} %get-tuple-element.18.refs_0_, ...), custom_call_target="tpu_custom_call" | custom-call | tf_op jit(solution)/shard_map/third/pallas_call | solution.py:219
  33.1 2.5 %rest.2 = (bf16[256,256]{1,0:T(8,128)(2,1)S(1)}, bf16[256,256]{1,0:T(8,128)(2,1)S(1)}) custom-call(s32[64,128]{1,0:T(8,128)S(1)} %get-tuple-element.16.packed, f32[128,128,256]{2,1,0:T(8,128)S(1)} %get-tuple-element.22.first, f32[128,128,256]{2,1,0:T(8,128)S(1)} %get-tuple-element.23.second, bf16[256,256]{1,0:T(8,128)(2,1)S(1)} %get-tuple-element.18.refs_0_, ...), custom_call_target="tpu_custom_call" | custom-call | tf_op jit(solution)/shard_map/rest/pallas_call | solution.py:238
  35.6 2.3 %collective-permute-start.15 = (bf16[256,256]{1,0:T(8,128)(2,1)S(1)}, bf16[256,256]{1,0:T(8,128)(2,1)S(1)}, u32[]{:S(2)}, u32[]{:S(2)}) collective-permute-start(bf16[256,256]{1,0:T(8,128)(2,1)S(1)} %get-tuple-element.25), channel_id=1, source_target_pairs={{0,4},{1,5},{2,6},{3,7},{4,0},{5,1},{6,2},{7,3},{8,12},{9,13},{10,... | collective-permute-start | bytes 393224 | tf_op jit(solution)/shard_map/ppermute | solution.py:283
  37.9 1.9 %rest.3 = bf16[256,256]{1,0:T(8,128)(2,1)S(1)} custom-call(s32[64,128]{1,0:T(8,128)S(1)} %get-tuple-element.16.packed, f32[128,128,256]{2,1,0:T(8,128)S(1)} %get-tuple-element.22.first, f32[128,128,256]{2,1,0:T(8,128)S(1)} %get-tuple-element.23.second, bf16[256,256]{1,0:T(8,128)(2,1)S(1)} %collective-permute-done.11.refs_12_.refs_0_), custom_call_target="tpu_custom_call" | custom-call | tf_op jit(solution)/shard_map/rest/pallas_call | solution.py:238
  39.7 2.4 %collective-permute-start.17 = (bf16[256,256]{1,0:T(8,128)(2,1)S(1)}, bf16[256,256]{1,0:T(8,128)(2,1)S(1)}, u32[]{:S(2)}, u32[]{:S(2)}) collective-permute-start(bf16[256,256]{1,0:T(8,128)(2,1)S(1)} %rest.3), channel_id=1, source_target_pairs={{0,12},{1,13},{2,14},{3,15},{4,8},{5,9},{6,10},{7,11},{8,4},{9,5},... | collective-permute-start | bytes 393224 | tf_op jit(solution)/shard_map/ppermute | solution.py:283
  42.1 0.0 collective-permute-start.16
  42.1 0.0 collective-permute-done.15.refs_1_
  42.1 5.9 %collective-permute-done.17.refs_3_ = bf16[256,256]{1,0:T(8,128)(2,1)S(1)} collective-permute-done((bf16[256,256]{1,0:T(8,128)(2,1)S(1)}, bf16[256,256]{1,0:T(8,128)(2,1)S(1)}, u32[]{:S(2)}, u32[]{:S(2)}) %collective-permute-start.17) | collective-permute-done | bytes 131104 | tf_op jit(solution)/shard_map/ppermute | solution.py:283
  48.0 5.3 %collective-permute-done.16.refs_2_ = bf16[256,256]{1,0:T(8,128)(2,1)S(1)} collective-permute-done((bf16[256,256]{1,0:T(8,128)(2,1)S(1)}, bf16[256,256]{1,0:T(8,128)(2,1)S(1)}, u32[]{:S(2)}, u32[]{:S(2)}) %collective-permute-start.16) | collective-permute-done | bytes 131104 | tf_op jit(solution)/shard_map/ppermute | solution.py:283
  53.4 1.2 %finish.1 = f32[2048,128]{1,0:T(8,128)} custom-call(bf16[256,256]{1,0:T(8,128)(2,1)S(1)} %get-tuple-element.24.refs_0_, bf16[256,256]{1,0:T(8,128)(2,1)S(1)} %collective-permute-done.15.refs_1_, bf16[256,256]{1,0:T(8,128)(2,1)S(1)} %collective-permute-done.16.refs_2_, bf16[256,256]{1,0:T(8,128)(2,1)S(1)} %collective-permute-done.17.refs_3_), custom_call_target="tpu_custom_call" | custom-call | tf_op jit(solution)/shard_map/finish/pallas_call | solution.py:265
Async XLA Ops:
  1.9 9.6 %collective-permute-start.3 = (bf16[256,256]{1,0:T(8,128)(2,1)S(1)}, bf16[256,256]{1,0:T(8,128)(2,1)S(1)}, u32[]{:S(2)}, u32[]{:S(2)}) collective-permute-start(bf16[256,256]{1,0:T(8,128)(2,1)S(1)} %get-tuple-element.19), channel_id=1, source_target_pairs={{0,4},{1,5},{2,6},{3,7},{4,0},{5,1},{6,2},{7,3},{8,12},{9,13},{10,... | collective-permute-start | bytes 393224 | tf_op jit(solution)/shard_map/ppermute | solution.py:283
  5.1 11.9 %collective-permute-start.7 = (bf16[256,256]{1,0:T(8,128)(2,1)S(1)}, bf16[256,256]{1,0:T(8,128)(2,1)S(1)}, u32[]{:S(2)}, u32[]{:S(2)}) collective-permute-start(bf16[256,256]{1,0:T(8,128)(2,1)S(1)} %get-tuple-element.20), channel_id=1, source_target_pairs={{0,8},{1,9},{2,10},{3,11},{4,12},{5,13},{6,14},{7,15},{8,0},{9,1},... | collective-permute-start | bytes 393224 | tf_op jit(solution)/shard_map/ppermute | solution.py:283
  9.7 7.2 %collective-permute-start.11 = (bf16[256,256]{1,0:T(8,128)(2,1)S(1)}, bf16[256,256]{1,0:T(8,128)(2,1)S(1)}, u32[]{:S(2)}, u32[]{:S(2)}) collective-permute-start(bf16[256,256]{1,0:T(8,128)(2,1)S(1)} %get-tuple-element.21), channel_id=1, source_target_pairs={{0,12},{1,13},{2,14},{3,15},{4,8},{5,9},{6,10},{7,11},{8,4},{9,5},... | collective-permute-start | bytes 393224 | tf_op jit(solution)/shard_map/ppermute | solution.py:283
  9.8 8.7 %collective-permute-start.1 = (bf16[256,256]{1,0:T(8,128)(2,1)S(1)}, bf16[256,256]{1,0:T(8,128)(2,1)S(1)}, u32[]{:S(2)}, u32[]{:S(2)}) collective-permute-start(bf16[256,256]{1,0:T(8,128)(2,1)S(1)} %get-tuple-element.18.refs_0_), channel_id=1, source_target_pairs={{0,2},{1,3},{2,0},{3,1},{4,6},{5,7},{6,4},{7,5},{8,10},{9,11},{10,... | collective-permute-start | bytes 393224 | tf_op jit(solution)/shard_map/ppermute | solution.py:283
  11.6 7.2 %collective-permute-start = (bf16[256,256]{1,0:T(8,128)(2,1)S(1)}, bf16[256,256]{1,0:T(8,128)(2,1)S(1)}, u32[]{:S(2)}, u32[]{:S(2)}) collective-permute-start(bf16[256,256]{1,0:T(8,128)(2,1)S(1)} %get-tuple-element.18.refs_0_), channel_id=1, source_target_pairs={{0,1},{1,0},{2,3},{3,2},{4,5},{5,4},{6,7},{7,6},{8,9},{9,8},{10,11... | collective-permute-start | bytes 393224 | tf_op jit(solution)/shard_map/ppermute | solution.py:283
  11.6 7.7 %collective-permute-start.5 = (bf16[256,256]{1,0:T(8,128)(2,1)S(1)}, bf16[256,256]{1,0:T(8,128)(2,1)S(1)}, u32[]{:S(2)}, u32[]{:S(2)}) collective-permute-start(bf16[256,256]{1,0:T(8,128)(2,1)S(1)} %collective-permute-done.3.refs_4_.refs_1_), channel_id=1, source_target_pairs={{0,2},{1,3},{2,0},{3,1},{4,6},{5,7},{6,4},{7,5},{8,10},{9,11},{10,... | collective-permute-start | bytes 393224 | tf_op jit(solution)/shard_map/ppermute | solution.py:283
  17.0 2.3 %collective-permute-start.4 = (bf16[256,256]{1,0:T(8,128)(2,1)S(1)}, bf16[256,256]{1,0:T(8,128)(2,1)S(1)}, u32[]{:S(2)}, u32[]{:S(2)}) collective-permute-start(bf16[256,256]{1,0:T(8,128)(2,1)S(1)} %collective-permute-done.3.refs_4_.refs_1_), channel_id=1, source_target_pairs={{0,1},{1,0},{2,3},{3,2},{4,5},{5,4},{6,7},{7,6},{8,9},{9,8},{10,11... | collective-permute-start | bytes 393224 | tf_op jit(solution)/shard_map/ppermute | solution.py:283
  17.0 6.4 %collective-permute-start.9 = (bf16[256,256]{1,0:T(8,128)(2,1)S(1)}, bf16[256,256]{1,0:T(8,128)(2,1)S(1)}, u32[]{:S(2)}, u32[]{:S(2)}) collective-permute-start(bf16[256,256]{1,0:T(8,128)(2,1)S(1)} %collective-permute-done.7.refs_8_), channel_id=1, source_target_pairs={{0,2},{1,3},{2,0},{3,1},{4,6},{5,7},{6,4},{7,5},{8,10},{9,11},{10,... | collective-permute-start | bytes 393224 | tf_op jit(solution)/shard_map/ppermute | solution.py:283
  18.5 4.9 %collective-permute-start.8 = (bf16[256,256]{1,0:T(8,128)(2,1)S(1)}, bf16[256,256]{1,0:T(8,128)(2,1)S(1)}, u32[]{:S(2)}, u32[]{:S(2)}) collective-permute-start(bf16[256,256]{1,0:T(8,128)(2,1)S(1)} %collective-permute-done.7.refs_8_), channel_id=1, source_target_pairs={{0,1},{1,0},{2,3},{3,2},{4,5},{5,4},{6,7},{7,6},{8,9},{9,8},{10,11... | collective-permute-start | bytes 393224 | tf_op jit(solution)/shard_map/ppermute | solution.py:283
  18.7 7.0 %collective-permute-start.13 = (bf16[256,256]{1,0:T(8,128)(2,1)S(1)}, bf16[256,256]{1,0:T(8,128)(2,1)S(1)}, u32[]{:S(2)}, u32[]{:S(2)}) collective-permute-start(bf16[256,256]{1,0:T(8,128)(2,1)S(1)} %collective-permute-done.11.refs_12_.refs_0_), channel_id=1, source_target_pairs={{0,2},{1,3},{2,0},{3,1},{4,6},{5,7},{6,4},{7,5},{8,10},{9,11},{10,... | collective-permute-start | bytes 393224 | tf_op jit(solution)/shard_map/ppermute | solution.py:283
  19.2 6.5 %collective-permute-start.12 = (bf16[256,256]{1,0:T(8,128)(2,1)S(1)}, bf16[256,256]{1,0:T(8,128)(2,1)S(1)}, u32[]{:S(2)}, u32[]{:S(2)}) collective-permute-start(bf16[256,256]{1,0:T(8,128)(2,1)S(1)} %collective-permute-done.11.refs_12_.refs_0_), channel_id=1, source_target_pairs={{0,1},{1,0},{2,3},{3,2},{4,5},{5,4},{6,7},{7,6},{8,9},{9,8},{10,11... | collective-permute-start | bytes 393224 | tf_op jit(solution)/shard_map/ppermute | solution.py:283
  19.2 6.5 %collective-permute-start.2 = (bf16[256,256]{1,0:T(8,128)(2,1)S(1)}, bf16[256,256]{1,0:T(8,128)(2,1)S(1)}, u32[]{:S(2)}, u32[]{:S(2)}) collective-permute-start(bf16[256,256]{1,0:T(8,128)(2,1)S(1)} %collective-permute-done.1.refs_2_), channel_id=1, source_target_pairs={{0,1},{1,0},{2,3},{3,2},{4,5},{5,4},{6,7},{7,6},{8,9},{9,8},{10,11... | collective-permute-start | bytes 393224 | tf_op jit(solution)/shard_map/ppermute | solution.py:283
  23.3 2.4 %collective-permute-start.6 = (bf16[256,256]{1,0:T(8,128)(2,1)S(1)}, bf16[256,256]{1,0:T(8,128)(2,1)S(1)}, u32[]{:S(2)}, u32[]{:S(2)}) collective-permute-start(bf16[256,256]{1,0:T(8,128)(2,1)S(1)} %collective-permute-done.5.refs_6_), channel_id=1, source_target_pairs={{0,1},{1,0},{2,3},{3,2},{4,5},{5,4},{6,7},{7,6},{8,9},{9,8},{10,11... | collective-permute-start | bytes 393224 | tf_op jit(solution)/shard_map/ppermute | solution.py:283
  23.3 2.4 %collective-permute-start.10 = (bf16[256,256]{1,0:T(8,128)(2,1)S(1)}, bf16[256,256]{1,0:T(8,128)(2,1)S(1)}, u32[]{:S(2)}, u32[]{:S(2)}) collective-permute-start(bf16[256,256]{1,0:T(8,128)(2,1)S(1)} %collective-permute-done.9.refs_10_), channel_id=1, source_target_pairs={{0,1},{1,0},{2,3},{3,2},{4,5},{5,4},{6,7},{7,6},{8,9},{9,8},{10,11... | collective-permute-start | bytes 393224 | tf_op jit(solution)/shard_map/ppermute | solution.py:283
  25.7 1.3 %collective-permute-start.14 = (bf16[256,256]{1,0:T(8,128)(2,1)S(1)}, bf16[256,256]{1,0:T(8,128)(2,1)S(1)}, u32[]{:S(2)}, u32[]{:S(2)}) collective-permute-start(bf16[256,256]{1,0:T(8,128)(2,1)S(1)} %collective-permute-done.13.refs_14_), channel_id=1, source_target_pairs={{0,1},{1,0},{2,3},{3,2},{4,5},{5,4},{6,7},{7,6},{8,9},{9,8},{10,11... | collective-permute-start | bytes 393224 | tf_op jit(solution)/shard_map/ppermute | solution.py:283
  35.6 6.5 %collective-permute-start.15 = (bf16[256,256]{1,0:T(8,128)(2,1)S(1)}, bf16[256,256]{1,0:T(8,128)(2,1)S(1)}, u32[]{:S(2)}, u32[]{:S(2)}) collective-permute-start(bf16[256,256]{1,0:T(8,128)(2,1)S(1)} %get-tuple-element.25), channel_id=1, source_target_pairs={{0,4},{1,5},{2,6},{3,7},{4,0},{5,1},{6,2},{7,3},{8,12},{9,13},{10,... | collective-permute-start | bytes 393224 | tf_op jit(solution)/shard_map/ppermute | solution.py:283
  39.7 8.3 %collective-permute-start.17 = (bf16[256,256]{1,0:T(8,128)(2,1)S(1)}, bf16[256,256]{1,0:T(8,128)(2,1)S(1)}, u32[]{:S(2)}, u32[]{:S(2)}) collective-permute-start(bf16[256,256]{1,0:T(8,128)(2,1)S(1)} %rest.3), channel_id=1, source_target_pairs={{0,12},{1,13},{2,14},{3,15},{4,8},{5,9},{6,10},{7,11},{8,4},{9,5},... | collective-permute-start | bytes 393224 | tf_op jit(solution)/shard_map/ppermute | solution.py:283
  42.1 11.3 %collective-permute-start.16 = (bf16[256,256]{1,0:T(8,128)(2,1)S(1)}, bf16[256,256]{1,0:T(8,128)(2,1)S(1)}, u32[]{:S(2)}, u32[]{:S(2)}) collective-permute-start(bf16[256,256]{1,0:T(8,128)(2,1)S(1)} %get-tuple-element.26), channel_id=1, source_target_pairs={{0,8},{1,9},{2,10},{3,11},{4,12},{5,13},{6,14},{7,15},{8,0},{9,1},... | collective-permute-start | bytes 393224 | tf_op jit(solution)/shard_map/ppermute | solution.py:283
